TPU v7x, 256 devices: a whole 4x4x8 slice. The times are simulated.
256 devices in a mesh: tok: 64 (over x, z, core), feat: 4 (over y).
Axes of the slice: x: 4, y: 4, z: 8, core: 2. Of those that a mesh axis runs over, the one named last changes fastest.
Arguments:
- queries: bfloat16 [8192, 4096], P('tok', 'feat'), may hold values from -12 to 12
- keys: bfloat16 [8192, 1024], P('tok', 'feat'), may hold values from -12 to 12
- values: bfloat16 [8192, 1024], P('tok', 'feat'), may hold values from -6 to 6
- out_weight: bfloat16 [4096, 4096], P('feat', 'tok'), may hold values from -0.09375 to 0.09375
- doc_lengths: int32 [6], replicated, may hold values from 1 to 5120, 8192 in all
Outputs:
- mixed: bfloat16 [8192, 4096], P('tok', 'feat')
Inputs may be any that keep to these rules, and one draw needn't show every extreme that they name: `doc_lengths`: the lengths sum to 8192, and the largest is exactly 5120.
All inputs are finite; a program needn't handle non-finite values.
Results may differ from a plain program's by a relative error of at most 0.012.
The roundings to bfloat16 on the way count: a program that leaves them out, or rounds other values in their place, can miss the bound.
Values may be sent and summed in bfloat16 or wider, within the bound.
A program may use at most 64 MiB of HBM per device.

v0:
```python
import jax
import jax.numpy as jnp
from jax import lax
from jax.sharding import PartitionSpec as P

HD = 128


ROPE_BASE = 500000.0
NEG_FILL = -1e30


def locate(token_index, doc_lengths):
    doc_ends = jnp.cumsum(doc_lengths)
    starts = doc_ends - doc_lengths
    doc_ids = jnp.sum((token_index[:, None] >= doc_ends[None, :]).astype(jnp.int32), axis=1)
    number = jnp.arange(doc_lengths.shape[0], dtype=jnp.int32)
    first_token = jnp.sum(
        jnp.where(doc_ids[:, None] == number[None, :], starts[None, :], 0), axis=1
    )
    return (doc_ids, token_index - first_token)


def rotary(tensor, positions):
    half_size = tensor.shape[-1] // 2
    frequency = ROPE_BASE ** (-(jnp.arange(half_size, dtype=jnp.float32) * 2.0 / tensor.shape[-1]))
    angles = positions.astype(jnp.float32)[:, None] * frequency[None, :]
    cosine = jnp.cos(angles)[:, None, :]
    sine_part = jnp.sin(angles)[:, None, :]
    first_half = tensor[..., :half_size]
    second_half = tensor[..., half_size:]
    return jnp.concatenate(
        [
            first_half * cosine - second_half * sine_part,
            second_half * cosine + first_half * sine_part,
        ],
        axis=-1,
    )


def pick_block(extent):
    for candidate in (512, 256, 128):
        return candidate
    return extent


def shards(queries, keys, values, out_weight, doc_lengths):
    my_index = lax.axis_index("tok")
    local_rows = queries.shape[0]
    local_heads = queries.shape[1] // HD
    kv_local = keys.shape[1] // HD
    group_size = local_heads // kv_local
    scale_factor = HD ** (-0.5)
    own_index = my_index * local_rows + jnp.arange(local_rows, dtype=jnp.int32)
    own_docs, own_positions = locate(own_index, doc_lengths)
    rotated_q = rotary(
        queries.astype(jnp.float32).reshape(local_rows, local_heads, HD), own_positions
    ).astype(jnp.bfloat16)
    rotated_k = rotary(
        keys.astype(jnp.float32).reshape(local_rows, kv_local, HD), own_positions
    ).astype(jnp.bfloat16)
    rotated_k = rotated_k.reshape(local_rows, kv_local * HD)

    def fresh(query_rows):
        running_max = jnp.full((kv_local, group_size, query_rows), NEG_FILL, jnp.float32)
        totals = jnp.zeros((kv_local, group_size, query_rows), jnp.float32)
        weighted = jnp.zeros((kv_local, group_size, query_rows, HD), jnp.float32)
        return (running_max, totals, weighted)

    def absorb(carry_state, query_block, query_index, key_piece, value_piece, offset):
        query_docs, query_positions = locate(query_index, doc_lengths)
        doc_begin = query_index[0] - query_positions[0]
        last_index = query_index[-1]
        extent = key_piece.shape[0]
        needed = (offset + extent > doc_begin) & (offset <= last_index)
        block_rows = pick_block(extent)

        def sweep_keys(state_in):

            def one_block(block_number, state_now):
                running_max, totals, weighted = state_now
                first_key = block_number * block_rows
                key_tile = lax.dynamic_slice_in_dim(key_piece, first_key, block_rows, 0).reshape(
                    block_rows, kv_local, HD
                )
                value_tile = lax.dynamic_slice_in_dim(
                    value_piece, first_key, block_rows, 0
                ).reshape(block_rows, kv_local, HD)
                key_index = first_key + jnp.arange(block_rows, dtype=jnp.int32)
                key_docs, key_positions = locate(key_index, doc_lengths)
                scores = (
                    jnp.einsum(
                        "qgjd,kgd->gjqk", query_block, key_tile, preferred_element_type=jnp.float32
                    )
                    * scale_factor
                )
                visible = (query_docs[:, None] == key_docs[None, :]) & (
                    key_index[None, :] <= query_index[:, None]
                )
                scores = jnp.where(visible, scores, NEG_FILL)
                new_max = jnp.maximum(running_max, jnp.max(scores, axis=-1))
                factor = jnp.exp(running_max - new_max)
                weights = jnp.where(visible, jnp.exp(scores - new_max[..., None]), 0.0)
                totals = totals * factor + jnp.sum(weights, axis=-1)
                update = jnp.einsum(
                    "gjqk,kgd->gjqd",
                    weights.astype(jnp.bfloat16),
                    value_tile,
                    preferred_element_type=jnp.float32,
                )
                weighted = weighted * factor[..., None] + update
                return (new_max, totals, weighted)

            return lax.fori_loop(0, extent // block_rows, one_block, state_in)

        return lax.cond(needed, sweep_keys, lambda state_in: state_in, carry_state)

    def finish(carry_state):
        running_max, totals, weighted = carry_state
        output = weighted / totals[..., None]
        query_rows = output.shape[2]
        return (
            output.transpose(2, 0, 1, 3).reshape(query_rows, local_heads * HD).astype(jnp.bfloat16)
        )

    groups = [(rotated_q, own_index)]
    query_sets = [
        (member[0].reshape(member[0].shape[0], kv_local, group_size, HD), member[1])
        for member in groups
    ]

    def fold_keys(states, pieces, offset):
        return tuple(
            (
                absorb(state_now, member[0], member[1], pieces[0], pieces[1], offset)
                for state_now, member in zip(states, query_sets)
            )
        )

    initial = tuple((fresh(member[0].shape[0]) for member in query_sets))
    states = fold_keys(
        initial,
        (
            lax.all_gather(rotated_k, "tok", axis=0, tiled=True),
            lax.all_gather(values, "tok", axis=0, tiled=True),
        ),
        jnp.int32(0),
    )
    results = [finish(state_now) for state_now in states]
    attended = results[0]
    partial_terms = jnp.dot(
        attended,
        lax.all_gather(out_weight, "tok", axis=1, tiled=True),
        preferred_element_type=jnp.float32,
    )
    return lax.psum_scatter(
        partial_terms.astype(jnp.bfloat16), "feat", scatter_dimension=1, tiled=True
    )


def solution(mesh):
    in_specs = (P("tok", "feat"), P("tok", "feat"), P("tok", "feat"), P("feat", "tok"), P())
    out_specs = P("tok", "feat")
    return jax.shard_map(shards, mesh=mesh, in_specs=in_specs, out_specs=out_specs, check_vma=False)
```

profile of v0, /device:TPU:4, one launch (start us, length us, event | category | flops | bytes accessed | tf_op | source)
XLA Modules:
  0.0 290.5 jit_solution(7119460857731323404)
XLA Ops:
  10.1 1.6 copy.40
  12.7 1.0 convert_bitcast_fusion
  16.3 73.4 %all-gather.4.cloned.1.call-done = bf16[8192,256]{0,1:T(8,128)(2,1)} async-done(((bf16[128,256]{0,1:T(8,128)(2,1)}), bf16[8192,256]{0,1:T(8,128)(2,1)}) %all-gather.4.cloned.1.call-update) | async-done | bytes 4194320 | tf_op jit(solution)/shard_map/all_gather | solution.py:144
  89.7 78.3 %all-gather.6.cloned.1.call-done = bf16[8192,256]{0,1:T(8,128)(2,1)} async-done(((bf16[128,256]{0,1:T(8,128)(2,1)}), bf16[8192,256]{0,1:T(8,128)(2,1)}) %all-gather.6.cloned.1.call-update) | async-done | bytes 4194320 | tf_op jit(solution)/shard_map/all_gather | solution.py:145
  168.0 75.7 %conditional.1 = (f32[2,4,128]{2,1,0:T(4,128)}, f32[2,4,128,128]{2,3,1,0:T(8,128)S(1)}) conditional(s32[]{:T(128)} %bitcast.3, () %tuple.34, (s32[6]{0:T(128)S(1)}, s32[128]{0:T(128)S(1)}, s32[128]{0:T(128)S(1)}, bf16[8192,256]{0,1:T(8,128)(2,1)}, bf16[128,2,4,128]{3,0,2,1:T(8,128)(2,1)S(1)}, /*index=5*/bf16[8192,256]{0,1:T(8,128)(2,1)}) %tuple.78), branch_computations={%region_3.4_spmd, %region_4.11_spmd} | conditional | flops 275855392 | bytes 10562971 | solution.py:116
  168.2 75.3 %while.19 = (s32[]{:T(128)}, f32[2,4,128]{2,1,0:T(4,128)S(1)}, f32[2,4,128]{2,1,0:T(4,128)}, f32[2,4,128,128]{3,2,1,0:T(8,128)S(1)}, s32[128]{0:T(128)S(1)}, /*i...) while((s32[]{:T(128)}, f32[2,4,128]{2,1,0:T(4,128)S(1)}, ...), condition=%wide.region_10.10_spmd.clone, body=%wide.region_6.9_spmd.clone.sunk | while | flops 275855360 | bytes 9514207 | solution.py:114
  168.2 1.1 constant_dynamic-slice_fusion.3
  171.3 0.9 convolution_add_fusion.2
  172.3 1.1 constant_dynamic-slice_fusion.3
  174.7 1.3 fusion.35
  176.0 0.9 convolution_add_fusion.2
  177.0 1.1 constant_dynamic-slice_fusion.3
  179.5 1.3 fusion.35
  180.8 0.9 convolution_add_fusion.2
  181.8 1.1 constant_dynamic-slice_fusion.3
  184.2 1.3 fusion.35
  186.5 1.1 constant_dynamic-slice_fusion.3
  189.0 1.3 fusion.35
  191.3 1.1 constant_dynamic-slice_fusion.3
  193.7 1.3 fusion.35
  195.0 0.9 convolution_add_fusion.2
  196.0 1.1 constant_dynamic-slice_fusion.3
  198.5 1.3 fusion.35
  199.8 0.9 convolution_add_fusion.2
  200.8 1.1 constant_dynamic-slice_fusion.3
  203.2 1.3 fusion.35
  205.5 1.1 constant_dynamic-slice_fusion.3
  208.0 1.3 fusion.35
  210.3 1.1 constant_dynamic-slice_fusion.3
  212.7 1.3 fusion.35
  214.0 0.9 convolution_add_fusion.2
  215.0 1.1 constant_dynamic-slice_fusion.3
  217.5 1.3 fusion.35
  219.7 1.1 constant_dynamic-slice_fusion.3
  222.2 1.3 fusion.35
  224.5 1.1 constant_dynamic-slice_fusion.3
  227.0 1.3 fusion.35
  228.3 0.9 convolution_add_fusion.2
  229.3 1.1 constant_dynamic-slice_fusion.3
  231.8 1.3 fusion.35
  233.1 0.9 convolution_add_fusion.2
  234.0 1.1 constant_dynamic-slice_fusion.3
  236.5 1.3 fusion.35
  238.8 1.1 constant_dynamic-slice_fusion.3
  241.3 1.3 fusion.35
  244.5 7.0 %all-gather.8.cloned.1.call-done = bf16[1024,4096]{0,1:T(8,128)(2,1)} async-done(((bf16[1024,64]{0,1:T(8,128)(2,1)}), bf16[1024,4096]{0,1:T(8,128)(2,1)}) %all-gather.8.cloned.1.call-update) | async-done | bytes 8388624 | tf_op jit(solution)/shard_map/all_gather | solution.py:153
  251.5 7.3 %convolution_convert_fusion = bf16[128,4096]{1,0:T(8,128)(2,1)} fusion(bf16[128,1024]{0,1:T(8,128)(2,1)S(1)} %bitcast.64, bf16[1024,4096]{0,1:T(8,128)(2,1)} %all-gather.8.cloned.1.call-done), kind=kOutput, calls=%fused_computation.23 | convolution fusion | flops 1074266112 | bytes 9699328 | tf_op jit(solution)/shard_map/dot_general | solution.py:151
  258.8 25.2 %reduce-scatter.2.cloned.1.call-done = bf16[128,1024]{1,0:T(8,128)(2,1)} async-done(((bf16[128,4096]{1,0:T(8,128)(2,1)}), bf16[128,1024]{1,0:T(8,128)(2,1)}) %reduce-scatter.2.cloned.1.call-update) | async-done | bytes 262160 | tf_op jit(solution)/shard_map/reduce_scatter | solution.py:156
  (155 shorter events, 36.9 us)
Async XLA Ops:
  6.5 83.2 %all-gather.4.cloned.1.call-start = ((), (), s32[]{:S(2)}) async-start(), calls=%async_computation.1 | async-start | bytes 4259840 | tf_op jit(solution)/shard_map/all_gather | solution.py:144
  10.1 158.0 %all-gather.6.cloned.1.call-start = ((), (), s32[]{:S(2)}) async-start(), calls=%async_computation.2 | async-start | bytes 4259840 | tf_op jit(solution)/shard_map/all_gather | solution.py:145
  11.7 239.8 %all-gather.8.cloned.1.call-start = ((), (), s32[]{:S(2)}) async-start(), calls=%async_computation.3 | async-start | bytes 8519680 | tf_op jit(solution)/shard_map/all_gather | solution.py:153
  12.4 271.6 %reduce-scatter.2.cloned.1.call-start = ((), (), s32[]{:S(2)}) async-start(), calls=%async_computation.4 | async-start | bytes 1310720 | tf_op jit(solution)/shard_map/reduce_scatter | solution.py:156
  15.7 152.3 %copy-start = (s32[6]{0:T(128)S(1)}, s32[6]{0:T(128)}, u32[]{:S(2)}) copy-start(s32[6]{0:T(128)} %param.13) | copy-start | bytes 76
Sparse Core Ops, SparseCore 0:
  10.2 79.5 all-gather.3
  92.3 75.6 all-gather.5
  170.8 80.6 all-gather.7
  258.9 25.0 reduce-scatter.1
where the time goes:
time: 292 us; the launch traced here: 291 us
  waiting for transfers between devices  185 us (63%)
  other arithmetic  38.1 us (13%)
  matrix products  31 us (11%)
  local copies, waits for them, and re-layouts  21.1 us (7%)
  between operations  14.5 us (5%)
    all_gather x1, waiting for transfers between devices, shards(): lax.all_gather(values, 'tok', axis=0, tiled=True)  78.3 us
    all_gather x1, waiting for transfers between devices, shards(): lax.all_gather(rotated_k, 'tok', axis=0, tiled=True)  73.4 us
    reduce_scatter x1, waiting for transfers between devices, shards(): lax.psum_scatter(partial_terms.astype(jnp.bfloat16), 'feat', scatter_dime...  25.2 us
    add x16, other arithmetic, one_block(): totals = totals * factor + jnp.sum(weights, axis=-1)  20.1 us
    dynamic_slice x16, local copies, waits for them, and re-layouts, one_block(): lax.dynamic_slice_in_dim(value_piece, first_key, block_rows, 0)  17.2 us
    dot_general x16, matrix products, one_block(): jnp.einsum('gjqk,kgd->gjqd', weights.astype(jnp.bfloat16), value_tile, pr...  15.1 us
    dot_general x16, matrix products, one_block(): jnp.einsum('qgjd,kgd->gjqk', query_block, key_tile, preferred_element_typ...  8.6 us
    reduce_sum x16, other arithmetic, one_block(): totals = totals * factor + jnp.sum(weights, axis=-1)  8.35 us
  transfers between devices with their start and end apart: 4, of which 4 were waited for; matrix products, arithmetic and copies ran while one was open for 27% of the time, Pallas kernels for 0%

commit v1 on v0

v1 whole, which is shorter than its diff:
```python
import functools

import jax
import jax.numpy as jnp
import numpy as np
from jax import lax
from jax.experimental import pallas as pl
from jax.experimental.pallas import tpu as pltpu
from jax.sharding import PartitionSpec as P

HD = 128
ROPE_BASE = 500000.0
LOW = -1e30
MASKED = -2e30
ROWS = 128
NX, NZ, NY = 4, 8, 4
FACTOR = float(HD**-0.5 * np.log2(np.e))
MESH = pl.DeviceIdType.MESH


def rotary_tables(doc_lengths):
    token = lax.axis_index("tok") * ROWS + lax.broadcasted_iota(jnp.int32, (ROWS, HD), 0)
    lane = lax.broadcasted_iota(jnp.int32, (ROWS, HD), 1)
    start = jnp.zeros((ROWS, HD), jnp.int32)
    end = jnp.int32(0)
    for number in range(doc_lengths.shape[0]):
        end = end + doc_lengths[number]
        start = jnp.where(token >= end, end, start)
    half = HD // 2
    frequency = (ROPE_BASE ** (-(np.arange(half, dtype=np.float64) * 2.0 / HD))).astype(np.float32)
    both = jnp.asarray(np.concatenate([frequency, frequency]))
    angles = (token - start).astype(jnp.float32) * both[None, :]
    sine = jnp.sin(angles)
    return jnp.cos(angles), jnp.where(lane < half, -sine, sine)


def kernel(
    q_in, k_in, v_in, w_in, cos_in, sin_in, len_ref, out_ref,
    q_stage, kv_stage, qbuf, kv, start_ref, m_ref, l_ref, acc_ref, own_att, att, wbuf, pbuf, part,
    a_s, a_r, q_s, q_r, z_s, z_r, sh_s, sh_r, g_s, g_r, w_s, w_r, wsh_s, wsh_r, e_s, e_r,
):
    t = lax.axis_index("tok")
    y = lax.axis_index("feat")
    x = t // 16
    z = (t // 2) % NZ
    c = t % 2

    def device(dx, dz, dc):
        return (((x + dx) % NX) * 16 + ((z + dz) % NZ) * 2 + (c + dc) % 2, y)

    sibling = device(0, 0, 1)

    barrier = pltpu.get_barrier_semaphore()
    count = 0

    def greet(who):
        pl.semaphore_signal(barrier, inc=1, device_id=who, device_id_type=MESH)

    for dx in range(NX):
        for dy in range(NY):
            if dx or dy:
                greet((((x + dx) % NX) * 16 + z * 2 + c, (y + dy) % NY))
                count += 1
        greet(device(dx, 0, 1))
        count += 1
    for dz in (1, NZ - 1):
        greet(device(0, dz, 0))
        count += 1

    def copy(src, dst, send, recv, who):
        return pltpu.make_async_remote_copy(
            src_ref=src, dst_ref=dst, send_sem=send, recv_sem=recv, device_id=who, device_id_type=MESH
        )

    cosine = cos_in[...]
    sine = sin_in[...]

    def rotate(block):
        wide = block.astype(jnp.float32)
        return (wide * cosine + pltpu.roll(wide, HD // 2, 1) * sine).astype(jnp.bfloat16)

    for head in range(2):
        columns = slice(head * HD, (head + 1) * HD)
        kv_stage[head, 0] = rotate(k_in[:, columns])
        kv_stage[head, 1] = v_in[:, columns]
    kv[x, z, c] = kv_stage[x // 2]

    pl.semaphore_wait(barrier, count)

    def x_copy(dx):
        to = (x + dx) % NX
        return copy(kv_stage.at[to // 2], kv.at[x, z, c], a_s.at[dx], a_r.at[dx], device(dx, 0, 0))

    def x_arrival(dx):
        slot = kv.at[(x + NX - dx) % NX, z, c]
        return copy(slot, slot, a_s.at[dx], a_r.at[dx], sibling)

    def order(j):
        return j + j // 2 - 2 * (j // 3)

    def block_of(j, r):
        return kv.at[(x + NX - order(j)) % NX, (z + r) % NZ, c]

    def ring_copy(j, r, to_r, dz):
        block = block_of(j, r)
        return copy(block, block, z_s.at[j, to_r], z_r.at[j, to_r], device(0, dz, 0))

    def share_copy(j, r):
        block = block_of(j, r)
        return copy(block, block, sh_s.at[j, r], sh_r.at[j, r], sibling)

    def share_arrival(j, r):
        block = kv.at[(x + NX - order(j)) % NX, (z + r) % NZ, 1 - c]
        return copy(block, block, sh_s.at[j, r], sh_r.at[j, r], sibling)

    for dx in (1, 3, 2):
        x_copy(dx).start()
    ring_copy(0, 0, 7, 1).start()
    ring_copy(0, 0, 1, NZ - 1).start()
    share_copy(0, 0).start()

    for head in range(8):
        q_stage[head] = rotate(q_in[:, head * HD : (head + 1) * HD])
    qbuf[x, c] = q_stage[2 * x + c]

    def q_copy(dx, dc):
        head = 2 * ((x + dx) % NX) + (c + dc) % 2
        return copy(q_stage.at[head], qbuf.at[x, c], q_s.at[dx, dc], q_r.at[dx, dc], device(dx, 0, dc))

    def q_arrival(dx, dc):
        slot = qbuf.at[(x + NX - dx) % NX, (c + dc) % 2]
        return copy(slot, slot, q_s.at[dx, dc], q_r.at[dx, dc], sibling)

    partners = [(0, 1), (1, 0), (1, 1), (3, 0), (3, 1), (2, 0), (2, 1)]
    for dx, dc in partners:
        q_copy(dx, dc).start()

    wbuf[z, c] = w_in[...]

    def w_copy(r, to_r, dz):
        block = wbuf.at[(z + r) % NZ, c]
        return copy(block, block, w_s.at[to_r], w_r.at[to_r], device(0, dz, 0))

    def w_share(r):
        block = wbuf.at[(z + r) % NZ, c]
        return copy(block, block, wsh_s.at[r], wsh_r.at[r], sibling)

    def w_share_arrival(r):
        block = wbuf.at[(z + r) % NZ, 1 - c]
        return copy(block, block, wsh_s.at[r], wsh_r.at[r], sibling)

    ends = []
    end = len_ref[0]
    for number in range(6):
        ends.append(end)
        if number < 5:
            end = end + len_ref[number + 1]
    row_iota = lax.broadcasted_iota(jnp.int32, (2 * ROWS, HD), 0)

    def prepare(row, _):
        token = row * (16 * ROWS) + z * (2 * ROWS) + row_iota
        start = jnp.zeros((2 * ROWS, HD), jnp.int32)
        for end in ends:
            start = jnp.where(token >= end, end, start)
        start_ref[row] = start
        m_ref[row] = jnp.full((2 * ROWS, HD), LOW, jnp.float32)
        l_ref[row] = jnp.zeros((2 * ROWS, HD), jnp.float32)
        acc_ref[row] = jnp.zeros((2 * ROWS, HD), jnp.float32)
        return 0

    lax.fori_loop(0, NX, prepare, 0)

    for j, dx in ((1, 1), (2, 3), (3, 2)):
        x_arrival(dx).wait_recv()
        ring_copy(j, 0, 7, 1).start()
        ring_copy(j, 0, 1, NZ - 1).start()
        share_copy(j, 0).start()

    def twice(value):
        return jnp.concatenate([value, value], axis=1)

    def attend(j, r):
        share_arrival(j, r).wait_recv()
        xk = (x + NX - order(j)) % NX
        zk = (z + r) % NZ
        key_first = xk * (16 * ROWS) + zk * (2 * ROWS)

        def one_row(row, _):
            apart = 8 * (row - xk) + z - zk

            @pl.when((apart >= 0) & (apart <= 20))
            def _():
                q = qbuf[row].reshape(2 * ROWS, HD)
                k = kv[xk, zk, :, 0].reshape(2 * ROWS, HD)
                v = kv[xk, zk, :, 1].reshape(2 * ROWS, HD)
                raw = lax.dot_general(
                    q, k, (((1,), (1,)), ((), ())), preferred_element_type=jnp.float32
                )
                key = key_first + lax.broadcasted_iota(jnp.int32, (2 * ROWS, 2 * ROWS), 1)
                token = (
                    row * (16 * ROWS)
                    + z * (2 * ROWS)
                    + lax.broadcasted_iota(jnp.int32, (2 * ROWS, 2 * ROWS), 0)
                )
                visible = (key >= twice(start_ref[row])) & (key <= token)
                raw = jnp.where(visible, raw, MASKED)
                old = m_ref[row]
                new = jnp.maximum(old, jnp.max(raw, axis=1, keepdims=True))
                shrink = jnp.exp2((old - new) * FACTOR)
                weights = jnp.exp2((raw - twice(new)) * FACTOR)
                l_ref[row] = l_ref[row] * shrink + jnp.sum(weights, axis=1, keepdims=True)
                acc_ref[row] = acc_ref[row] * shrink + jnp.dot(
                    weights.astype(jnp.bfloat16), v, preferred_element_type=jnp.float32
                )
                m_ref[row] = new

            return 0

        lax.fori_loop(xk, NX, one_row, 0)

    def item(m):
        d = 1 + m // 8
        j = (m // 2) % 4
        s = m % 2
        return d, j, s, (1 - s) * (NZ - d) + s * d

    def arrive(m):
        d, j, s, r = item(m)
        block = block_of(j, r)
        copy(block, block, z_s.at[j, r], z_r.at[j, r], sibling).wait_recv()

        @pl.when((d < 3) | (c == s))
        def _():
            ring_copy(j, r, r - 1 + 2 * s, (1 + 6 * s)).start()

        share_copy(j, r).start()

    def first_items(m, _):
        arrive(m)
        attend(m, 0)
        return 0

    def middle_items(m, _):
        arrive(m)
        _, j, _, r = item(m - 4)
        attend(j, r)
        return 0

    def last_items(m, _):
        block = block_of(m, 4)
        copy(block, block, z_s.at[m, 4], z_r.at[m, 4], sibling).wait_recv()
        share_copy(m, 4).start()
        _, j, _, r = item(m + 20)
        attend(j, r)
        return 0

    def final_items(m, _):
        attend(m, 4)
        return 0

    for dx, dc in partners:
        q_arrival(dx, dc).wait_recv()
    lax.fori_loop(0, 4, first_items, 0)
    lax.fori_loop(4, 24, middle_items, 0)

    w_copy(0, 7, 1).start()
    w_copy(0, 1, NZ - 1).start()
    w_share(0).start()

    lax.fori_loop(0, 4, last_items, 0)
    lax.fori_loop(0, 4, final_items, 0)

    def finish(row, _):
        done = (acc_ref[row] / l_ref[row]).astype(jnp.bfloat16)
        own_att[0, row] = done[:ROWS]
        own_att[1, row] = done[ROWS:]
        return 0

    lax.fori_loop(0, NX, finish, 0)

    def g_copy(dx, dc):
        return copy(
            own_att.at[(c + dc) % 2], att.at[2 * x + c], g_s.at[dx, dc], g_r.at[dx, dc], device(dx, 0, dc)
        )

    def g_arrival(dx, dc):
        slot = att.at[2 * ((x + NX - dx) % NX) + (c + dc) % 2]
        return copy(slot, slot, g_s.at[dx, dc], g_r.at[dx, dc], sibling)

    for dx, dc in partners:
        g_copy(dx, dc).start()
    att[2 * x + c] = own_att[c]

    def w_step(n, _):
        d = 1 + n // 2
        s = n % 2
        r = (1 - s) * (NZ - d) + s * d
        block = wbuf.at[(z + r) % NZ, c]
        copy(block, block, w_s.at[r], w_r.at[r], sibling).wait_recv()

        @pl.when((d < 3) | (c == s))
        def _():
            w_copy(r, r - 1 + 2 * s, 1 + 6 * s).start()

        w_share(r).start()
        return 0

    lax.fori_loop(0, 6, w_step, 0)
    last_w = wbuf.at[(z + 4) % NZ, c]
    copy(last_w, last_w, w_s.at[4], w_r.at[4], sibling).wait_recv()
    w_share(4).start()

    for dx, dc in partners:
        g_arrival(dx, dc).wait_recv()

    def w_wait(r, _):
        w_share_arrival(r).wait_recv()
        return 0

    lax.fori_loop(0, NZ, w_wait, 0)

    def e_copy(row, nb):
        return copy(
            pbuf.at[row, nb], part.at[y, nb], e_s.at[row, nb], e_r.at[y, nb], (row * 16 + z * 2 + c, x)
        )

    def project(nb, _):
        left = jnp.concatenate([att[head].reshape(4 * ROWS, HD) for head in range(8)], axis=1)
        right = wbuf[pl.ds(2 * nb, 2)].reshape(2 * HD, 8 * HD)
        product = lax.dot_general(
            left, right, (((1,), (1,)), ((), ())), preferred_element_type=jnp.float32
        ).astype(jnp.bfloat16)
        for row in range(NX):
            pbuf[row, nb] = product[row * ROWS : (row + 1) * ROWS]
        for row in range(NX):
            mine = (x == row) & (y == x)

            @pl.when(mine)
            def _():
                part[y, nb] = pbuf[row, nb]

            @pl.when(jnp.logical_not(mine))
            def _():
                e_copy(row, nb).start()

        return 0

    lax.fori_loop(0, 4, project, 0)

    for nb in range(4):
        for source in range(NY):
            slot = part.at[source, nb]
            arrival = copy(slot, slot, e_s.at[source, nb], e_r.at[source, nb], sibling)

            @pl.when(jnp.logical_not((x == y) & (source == y)))
            def _():
                arrival.wait_recv()

        total = part[0, nb].astype(jnp.float32)
        for source in range(1, NY):
            total = total + part[source, nb].astype(jnp.float32)
        out_ref[:, nb * 256 : (nb + 1) * 256] = total.astype(jnp.bfloat16)

    for dx in (1, 3, 2):
        x_copy(dx).wait_send()
    for dx, dc in partners:
        q_copy(dx, dc).wait_send()
        g_copy(dx, dc).wait_send()

    def sent(n, _):
        j = n % 4
        r = n // 4
        share_copy(j, r).wait_send()
        return 0

    lax.fori_loop(0, 32, sent, 0)

    def ring_sent(n, _):
        j = n % 4
        r = 1 + n // 4
        block = block_of(j, r)
        copy(block, block, z_s.at[j, r], z_r.at[j, r], sibling).wait_send()
        return 0

    lax.fori_loop(0, 28, ring_sent, 0)

    def w_sent(r, _):
        w_share(r).wait_send()
        return 0

    lax.fori_loop(0, NZ, w_sent, 0)

    def w_ring_sent(r, _):
        block = wbuf.at[(z + r) % NZ, c]
        copy(block, block, w_s.at[r], w_r.at[r], sibling).wait_send()
        return 0

    lax.fori_loop(1, NZ, w_ring_sent, 0)
    for row in range(NX):
        mine = (x == row) & (y == x)

        @pl.when(jnp.logical_not(mine))
        def _():
            for nb in range(4):
                e_copy(row, nb).wait_send()


def shards(queries, keys, values, out_weight, doc_lengths):
    cosine, sine = rotary_tables(doc_lengths)
    vmem = pl.BlockSpec(memory_space=pltpu.VMEM)
    bf16, f32 = jnp.bfloat16, jnp.float32
    dma = pltpu.SemaphoreType.DMA
    return pl.pallas_call(
        kernel,
        out_shape=jax.ShapeDtypeStruct((ROWS, 1024), bf16),
        in_specs=[vmem] * 6 + [pl.BlockSpec(memory_space=pltpu.SMEM)],
        out_specs=vmem,
        scratch_shapes=[
            pltpu.VMEM((8, ROWS, HD), bf16),
            pltpu.VMEM((2, 2, ROWS, HD), bf16),
            pltpu.VMEM((NX, 2, ROWS, HD), bf16),
            pltpu.VMEM((NX, NZ, 2, 2, ROWS, HD), bf16),
            pltpu.VMEM((NX, 2 * ROWS, HD), jnp.int32),
            pltpu.VMEM((NX, 2 * ROWS, HD), f32),
            pltpu.VMEM((NX, 2 * ROWS, HD), f32),
            pltpu.VMEM((NX, 2 * ROWS, HD), f32),
            pltpu.VMEM((2, NX, ROWS, HD), bf16),
            pltpu.VMEM((8, NX, ROWS, HD), bf16),
            pltpu.VMEM((NZ, 2, 64, 1024), bf16),
            pltpu.VMEM((NX, 4, ROWS, 256), bf16),
            pltpu.VMEM((NY, 4, ROWS, 256), bf16),
            dma((4,)), dma((4,)),
            dma((4, 2)), dma((4, 2)),
            dma((4, 8)), dma((4, 8)),
            dma((4, 8)), dma((4, 8)),
            dma((4, 2)), dma((4, 2)),
            dma((8,)), dma((8,)),
            dma((8,)), dma((8,)),
            dma((4, 4)), dma((4, 4)),
        ],
        compiler_params=pltpu.CompilerParams(
            collective_id=0, has_side_effects=True, vmem_limit_bytes=48 << 20
        ),
    )(queries, keys, values, out_weight.T, cosine, sine, doc_lengths)


def solution(mesh):
    in_specs = (P("tok", "feat"), P("tok", "feat"), P("tok", "feat"), P("feat", "tok"), P())
    return jax.shard_map(
        shards, mesh=mesh, in_specs=in_specs, out_specs=P("tok", "feat"), check_vma=False
    )
```

time: 292 us -> 90.5 us (0.31)
  waiting for transfers between devices: 185 us -> 0 us
  Pallas kernels: 0 us -> 80 us
  other arithmetic: 38.1 us -> 1.76 us
  matrix products: 31 us -> 0 us
  local copies, waits for them, and re-layouts: 21.1 us -> 4.67 us
  between operations: 14.5 us -> 3.81 us
    all_gather x3 -> x0, waiting for transfers between devices: 159 us -> none  [the longest x1 78.3 us: shards(): lax.all_gather(values, 'tok', axis=0, tiled=True)]
    pallas_call x0 -> x1, Pallas kernels: none -> 80 us  [shards(): pl.pallas_call(kernel, out_shape=jax.ShapeDtypeStruct((ROWS, 1024), bf16)...]
    dot_general x33 -> x0, matrix products: 31 us -> none  [the longest x16 15.1 us: one_block(): jnp.einsum('gjqk,kgd->gjqd', weights.astype(jnp.bfloat16), value_tile, pr...]
    reduce_scatter x1 -> x0, waiting for transfers between devices: 25.2 us -> none  [shards(): lax.psum_scatter(partial_terms.astype(jnp.bfloat16), 'feat', scatter_dime...]
    add x33 -> x0, other arithmetic: 20.2 us -> none  [the longest x16 20.1 us: one_block(): totals = totals * factor + jnp.sum(weights, axis=-1)]
    dynamic_slice x16 -> x0, local copies, waits for them, and re-layouts: 17.2 us -> none  [one_block(): lax.dynamic_slice_in_dim(value_piece, first_key, block_rows, 0)]
    reduce_sum x34 -> x0, other arithmetic: 9.9 us -> none  [the longest x16 8.35 us: one_block(): totals = totals * factor + jnp.sum(weights, axis=-1)]
    and x16 -> x0, other arithmetic: 3.27 us -> none  [one_block(): (query_docs[:, None] == key_docs[None, :]) & (key_index[None, :] <= query...]
  transfers between devices with their start and end apart: 4 -> 0, of which waited for: 4 -> 0; matrix products, arithmetic and copies ran while one was open for 27% -> 0% of each run, Pallas kernels for 0% -> 0%
where the time goes in v1:
time: 90.5 us; the launch traced here: 90.2 us
  Pallas kernels  80 us (88%)
  local copies, waits for them, and re-layouts  4.67 us (5%)
  between operations  3.81 us (4%)
  other arithmetic  1.76 us (2%)
    pallas_call x1, Pallas kernels, shards(): pl.pallas_call(kernel, out_shape=jax.ShapeDtypeStruct((ROWS, 1024), bf16)...  80 us
    unnamed x11, local copies, waits for them, and re-layouts  3.13 us

profile of v1, /device:TPU:4, one launch (start us, length us, event | category | flops | bytes accessed | tf_op | source)
XLA Modules:
  0.0 90.2 jit_solution(9681156655296425437)
XLA Ops:
  0.0 0.0 copy-start.1
  0.0 1.5 %fusion.1 = (s32[1]{0:T(128)}, s32[1]{0:T(128)}, s32[1]{0:T(128)}, s32[1]{0:T(128)}, s32[1]{0:T(128)}, /*index=5*/s32[1]{0:T(128)}) fusion(s32[6]{0:T(128)} %len_ref.1), kind=kLoop, calls=%fused_computation.11 | loop fusion | bytes 48 | tf_op jit(solution)/shard_map/slice | solution.py:27
  5.3 0.6 compare_select_fusion
  6.0 0.0 copy-start.2
  6.0 1.1 %negate_select_fusion = (f32[128,128]{1,0:T(8,128)S(1)}, f32[128,128]{1,0:T(8,128)S(1)}) fusion(f32[128]{0:T(128)} %constant.14.clone, s32[128]{0:T(128)S(1)} %get-tuple-element.13, s32[]{:T(128)S(6)} %add.24, s32[]{:T(128)S(6)} %add.25, s32[]{:T(128)S(6)} %add.26, s32[]{:T(128)S(6)} %add.27, s32[]{:T(128)S(6)} %add.28, s32[128]{0:T(128)S(1)} %get-tuple-element.14, ...), kind=kLoop, calls=%fused_computation | loop fusion | flops 163840 | bytes 133396 | tf_op jit(solution)/shard_map/jit(_where)/select_n | solution.py:34
  7.1 0.0 copy-start.4
  7.1 0.0 copy-done.1
  7.1 0.0 copy-done.2
  7.1 0.6 copy-done.4
  7.7 0.0 copy-start
  7.7 0.9 %copy-done = bf16[128,1024]{1,0:T(8,128)(2,1)S(1)} copy-done((bf16[128,1024]{1,0:T(8,128)(2,1)S(1)}, bf16[128,1024]{1,0:T(8,128)(2,1)}, u32[]{:S(2)}) %copy-start) | copy-done | bytes 262168
  8.7 0.0 copy-start.3
  8.7 0.8 copy-done.3
  9.5 80.0 %shard_map.64 = bf16[128,1024]{1,0:T(8,128)(2,1)S(1)} custom-call(bf16[128,1024]{1,0:T(8,128)(2,1)S(1)} %copy-done, bf16[128,256]{1,0:T(8,128)(2,1)S(1)} %copy-done.2, bf16[128,256]{1,0:T(8,128)(2,1)S(1)} %copy-done.3, bf16[64,1024]{1,0:T(8,128)(2,1)S(1)} %bitcast.7, f32[128,128]{1,0:T(8,128)S(1)} %get-tuple-element.6.cos_in, ...), custom_call_target="tpu_custom_call" | custom-call | tf_op jit(solution)/shard_map/pallas_call | solution.py:413
  89.5 0.7 copy.8
  (3 shorter events, 0.0 us)
Async XLA Ops:
  0.0 7.1 %copy-start.1 = (bf16[1024,64]{0,1:T(8,128)(2,1)S(1)}, bf16[1024,64]{0,1:T(8,128)(2,1)}, u32[]{:S(2)}) copy-start(bf16[1024,64]{0,1:T(8,128)(2,1)} %param.9) | copy-start | bytes 393220
  6.0 1.2 %copy-start.2 = (bf16[128,256]{1,0:T(8,128)(2,1)S(1)}, bf16[128,256]{1,0:T(8,128)(2,1)}, u32[]{:S(2)}) copy-start(bf16[128,256]{1,0:T(8,128)(2,1)} %k_in.1) | copy-start | bytes 196612
  7.1 0.7 copy-start.4
  7.7 0.9 %copy-start = (bf16[128,1024]{1,0:T(8,128)(2,1)S(1)}, bf16[128,1024]{1,0:T(8,128)(2,1)}, u32[]{:S(2)}) copy-start(bf16[128,1024]{1,0:T(8,128)(2,1)} %q_in.1) | copy-start | bytes 786436
  8.7 0.8 copy-start.3

commit v2 on v1

--- a/solution.py
+++ b/solution.py
@@ -18,25 +18,15 @@
 MESH = pl.DeviceIdType.MESH
 
 
-def rotary_tables(doc_lengths):
-    token = lax.axis_index("tok") * ROWS + lax.broadcasted_iota(jnp.int32, (ROWS, HD), 0)
-    lane = lax.broadcasted_iota(jnp.int32, (ROWS, HD), 1)
-    start = jnp.zeros((ROWS, HD), jnp.int32)
-    end = jnp.int32(0)
-    for number in range(doc_lengths.shape[0]):
-        end = end + doc_lengths[number]
-        start = jnp.where(token >= end, end, start)
+def frequencies():
     half = HD // 2
-    frequency = (ROPE_BASE ** (-(np.arange(half, dtype=np.float64) * 2.0 / HD))).astype(np.float32)
-    both = jnp.asarray(np.concatenate([frequency, frequency]))
-    angles = (token - start).astype(jnp.float32) * both[None, :]
-    sine = jnp.sin(angles)
-    return jnp.cos(angles), jnp.where(lane < half, -sine, sine)
+    frequency = ROPE_BASE ** (-(np.arange(half, dtype=np.float64) * 2.0 / HD))
+    return np.concatenate([frequency, frequency]).astype(np.float32).reshape(1, HD)
 
 
 def kernel(
-    q_in, k_in, v_in, w_in, cos_in, sin_in, len_ref, out_ref,
-    q_stage, kv_stage, qbuf, kv, start_ref, m_ref, l_ref, acc_ref, own_att, att, wbuf, pbuf, part,
+    q_hbm, k_hbm, v_hbm, w_hbm, freq_ref, len_ref, out_ref,
+    q_in, k_in, v_in, in_sem, q_stage, kv_stage, qbuf, kv, start_ref, m_ref, l_ref, acc_ref, own_att, att, wbuf, pbuf, part,
     a_s, a_r, q_s, q_r, z_s, z_r, sh_s, sh_r, g_s, g_r, w_s, w_r, wsh_s, wsh_r, e_s, e_r,
 ):
     t = lax.axis_index("tok")
@@ -49,6 +39,15 @@
         return (((x + dx) % NX) * 16 + ((z + dz) % NZ) * 2 + (c + dc) % 2, y)
 
     sibling = device(0, 0, 1)
+
+    loads = [
+        pltpu.make_async_copy(k_hbm, k_in, in_sem.at[0]),
+        pltpu.make_async_copy(v_hbm, v_in, in_sem.at[1]),
+        pltpu.make_async_copy(q_hbm, q_in, in_sem.at[2]),
+        pltpu.make_async_copy(w_hbm, wbuf.at[z, c], in_sem.at[3]),
+    ]
+    for load in loads:
+        load.start()
 
     barrier = pltpu.get_barrier_semaphore()
     count = 0
@@ -72,16 +71,33 @@
             src_ref=src, dst_ref=dst, send_sem=send, recv_sem=recv, device_id=who, device_id_type=MESH
         )
 
-    cosine = cos_in[...]
-    sine = sin_in[...]
+    ends = []
+    end = len_ref[0]
+    for number in range(5):
+        ends.append(end)
+        end = end + len_ref[number + 1]
+
+    def first_token(token):
+        start = jnp.zeros(token.shape, jnp.int32)
+        for end in ends:
+            start = jnp.where(token >= end, end, start)
+        return start
+
+    token = t * ROWS + lax.broadcasted_iota(jnp.int32, (ROWS, HD), 0)
+    angles = (token - first_token(token)).astype(jnp.float32) * freq_ref[...]
+    cosine = jnp.cos(angles)
+    sine = jnp.sin(angles)
+    sine = jnp.where(lax.broadcasted_iota(jnp.int32, (ROWS, HD), 1) < HD // 2, -sine, sine)
 
     def rotate(block):
         wide = block.astype(jnp.float32)
-        return (wide * cosine + pltpu.roll(wide, HD // 2, 1) * sine).astype(jnp.bfloat16)
-
+        return wide * cosine + pltpu.roll(wide, HD // 2, 1) * sine
+
+    loads[0].wait()
+    loads[1].wait()
     for head in range(2):
         columns = slice(head * HD, (head + 1) * HD)
-        kv_stage[head, 0] = rotate(k_in[:, columns])
+        kv_stage[head, 0] = rotate(k_in[:, columns]).T.astype(jnp.bfloat16)
         kv_stage[head, 1] = v_in[:, columns]
     kv[x, z, c] = kv_stage[x // 2]
 
@@ -112,15 +128,32 @@
     def share_arrival(j, r):
         block = kv.at[(x + NX - order(j)) % NX, (z + r) % NZ, 1 - c]
         return copy(block, block, sh_s.at[j, r], sh_r.at[j, r], sibling)
+
+    def w_copy(r, to_r, dz):
+        block = wbuf.at[(z + r) % NZ, c]
+        return copy(block, block, w_s.at[to_r], w_r.at[to_r], device(0, dz, 0))
+
+    def w_share(r):
+        block = wbuf.at[(z + r) % NZ, c]
+        return copy(block, block, wsh_s.at[r], wsh_r.at[r], sibling)
+
+    def w_share_arrival(r):
+        block = wbuf.at[(z + r) % NZ, 1 - c]
+        return copy(block, block, wsh_s.at[r], wsh_r.at[r], sibling)
 
     for dx in (1, 3, 2):
         x_copy(dx).start()
     ring_copy(0, 0, 7, 1).start()
     ring_copy(0, 0, 1, NZ - 1).start()
     share_copy(0, 0).start()
+    loads[3].wait()
+    w_copy(0, 7, 1).start()
+    w_copy(0, 1, NZ - 1).start()
+    w_share(0).start()
+    loads[2].wait()
 
     for head in range(8):
-        q_stage[head] = rotate(q_in[:, head * HD : (head + 1) * HD])
+        q_stage[head] = rotate(q_in[:, head * HD : (head + 1) * HD]).astype(jnp.bfloat16)
     qbuf[x, c] = q_stage[2 * x + c]
 
     def q_copy(dx, dc):
@@ -135,34 +168,11 @@
     for dx, dc in partners:
         q_copy(dx, dc).start()
 
-    wbuf[z, c] = w_in[...]
-
-    def w_copy(r, to_r, dz):
-        block = wbuf.at[(z + r) % NZ, c]
-        return copy(block, block, w_s.at[to_r], w_r.at[to_r], device(0, dz, 0))
-
-    def w_share(r):
-        block = wbuf.at[(z + r) % NZ, c]
-        return copy(block, block, wsh_s.at[r], wsh_r.at[r], sibling)
-
-    def w_share_arrival(r):
-        block = wbuf.at[(z + r) % NZ, 1 - c]
-        return copy(block, block, wsh_s.at[r], wsh_r.at[r], sibling)
-
-    ends = []
-    end = len_ref[0]
-    for number in range(6):
-        ends.append(end)
-        if number < 5:
-            end = end + len_ref[number + 1]
     row_iota = lax.broadcasted_iota(jnp.int32, (2 * ROWS, HD), 0)
 
     def prepare(row, _):
         token = row * (16 * ROWS) + z * (2 * ROWS) + row_iota
-        start = jnp.zeros((2 * ROWS, HD), jnp.int32)
-        for end in ends:
-            start = jnp.where(token >= end, end, start)
-        start_ref[row] = start
+        start_ref[row] = first_token(token)
         m_ref[row] = jnp.full((2 * ROWS, HD), LOW, jnp.float32)
         l_ref[row] = jnp.zeros((2 * ROWS, HD), jnp.float32)
         acc_ref[row] = jnp.zeros((2 * ROWS, HD), jnp.float32)
@@ -176,47 +186,63 @@
         ring_copy(j, 0, 1, NZ - 1).start()
         share_copy(j, 0).start()
 
-    def twice(value):
-        return jnp.concatenate([value, value], axis=1)
-
-    def attend(j, r):
-        share_arrival(j, r).wait_recv()
-        xk = (x + NX - order(j)) % NX
+    def attend_rows(rows, r):
         zk = (z + r) % NZ
-        key_first = xk * (16 * ROWS) + zk * (2 * ROWS)
-
-        def one_row(row, _):
-            apart = 8 * (row - xk) + z - zk
-
-            @pl.when((apart >= 0) & (apart <= 20))
-            def _():
-                q = qbuf[row].reshape(2 * ROWS, HD)
-                k = kv[xk, zk, :, 0].reshape(2 * ROWS, HD)
-                v = kv[xk, zk, :, 1].reshape(2 * ROWS, HD)
-                raw = lax.dot_general(
-                    q, k, (((1,), (1,)), ((), ())), preferred_element_type=jnp.float32
-                )
-                key = key_first + lax.broadcasted_iota(jnp.int32, (2 * ROWS, 2 * ROWS), 1)
-                token = (
-                    row * (16 * ROWS)
-                    + z * (2 * ROWS)
-                    + lax.broadcasted_iota(jnp.int32, (2 * ROWS, 2 * ROWS), 0)
-                )
-                visible = (key >= twice(start_ref[row])) & (key <= token)
-                raw = jnp.where(visible, raw, MASKED)
-                old = m_ref[row]
-                new = jnp.maximum(old, jnp.max(raw, axis=1, keepdims=True))
-                shrink = jnp.exp2((old - new) * FACTOR)
-                weights = jnp.exp2((raw - twice(new)) * FACTOR)
-                l_ref[row] = l_ref[row] * shrink + jnp.sum(weights, axis=1, keepdims=True)
-                acc_ref[row] = acc_ref[row] * shrink + jnp.dot(
-                    weights.astype(jnp.bfloat16), v, preferred_element_type=jnp.float32
-                )
-                m_ref[row] = new
-
-            return 0
-
-        lax.fori_loop(xk, NX, one_row, 0)
+        lane = lax.broadcasted_iota(jnp.int32, (2 * ROWS, HD), 1)
+        keys = [
+            jnp.concatenate([kv[xk, zk, 0, 0], kv[xk, zk, 1, 0]], axis=1)
+            for xk in range(max(rows) + 1)
+        ]
+        scores = []
+        for row in rows:
+            q = qbuf[row].reshape(2 * ROWS, HD)
+            scores.append(
+                [jnp.dot(q, keys[xk], preferred_element_type=jnp.float32) for xk in range(row + 1)]
+            )
+        for row, raws in zip(rows, scores):
+            start = start_ref[row]
+            token = row * (16 * ROWS) + z * (2 * ROWS) + row_iota
+            pieces = []
+            for xk, raw in enumerate(raws):
+                for side in range(2):
+                    key = xk * (16 * ROWS) + zk * (2 * ROWS) + side * HD + lane
+                    visible = key >= start
+                    if xk == row:
+                        visible = visible & (key <= token)
+                    piece = raw[:, side * HD : (side + 1) * HD]
+                    pieces.append(jnp.where(visible, piece, MASKED))
+            old = m_ref[row]
+            new = jnp.maximum(
+                old, jnp.max(functools.reduce(jnp.maximum, pieces), axis=1, keepdims=True)
+            )
+            shrink = jnp.exp2((old - new) * FACTOR)
+            weights = [jnp.exp2((piece - new) * FACTOR) for piece in pieces]
+            m_ref[row] = new
+            l_ref[row] = l_ref[row] * shrink + functools.reduce(jnp.add, weights)
+            v = kv[0 : row + 1, zk, :, 1].reshape((row + 1) * 2 * ROWS, HD)
+            acc_ref[row] = acc_ref[row] * shrink + jnp.dot(
+                jnp.concatenate([weight.astype(jnp.bfloat16) for weight in weights], axis=1),
+                v,
+                preferred_element_type=jnp.float32,
+            )
+
+    def attend_unit(unit, _):
+        group = unit // 2
+        odd = group % 2
+        d = (group + 1) // 2
+        r = odd * (NZ - d) + (1 - odd) * d
+
+        @pl.when(unit % 2 == 0)
+        def _():
+            for j in range(4):
+                share_arrival(j, r).wait_recv()
+            attend_rows((0, 3), r)
+
+        @pl.when(unit % 2 == 1)
+        def _():
+            attend_rows((1, 2), r)
+
+        return 0
 
     def item(m):
         d = 1 + m // 8
@@ -235,63 +261,15 @@
 
         share_copy(j, r).start()
 
-    def first_items(m, _):
-        arrive(m)
-        attend(m, 0)
-        return 0
-
-    def middle_items(m, _):
-        arrive(m)
-        _, j, _, r = item(m - 4)
-        attend(j, r)
-        return 0
-
-    def last_items(m, _):
-        block = block_of(m, 4)
-        copy(block, block, z_s.at[m, 4], z_r.at[m, 4], sibling).wait_recv()
-        share_copy(m, 4).start()
-        _, j, _, r = item(m + 20)
-        attend(j, r)
-        return 0
-
-    def final_items(m, _):
-        attend(m, 4)
-        return 0
-
-    for dx, dc in partners:
-        q_arrival(dx, dc).wait_recv()
-    lax.fori_loop(0, 4, first_items, 0)
-    lax.fori_loop(4, 24, middle_items, 0)
-
-    w_copy(0, 7, 1).start()
-    w_copy(0, 1, NZ - 1).start()
-    w_share(0).start()
-
-    lax.fori_loop(0, 4, last_items, 0)
-    lax.fori_loop(0, 4, final_items, 0)
-
-    def finish(row, _):
-        done = (acc_ref[row] / l_ref[row]).astype(jnp.bfloat16)
-        own_att[0, row] = done[:ROWS]
-        own_att[1, row] = done[ROWS:]
-        return 0
-
-    lax.fori_loop(0, NX, finish, 0)
-
-    def g_copy(dx, dc):
-        return copy(
-            own_att.at[(c + dc) % 2], att.at[2 * x + c], g_s.at[dx, dc], g_r.at[dx, dc], device(dx, 0, dc)
-        )
-
-    def g_arrival(dx, dc):
-        slot = att.at[2 * ((x + NX - dx) % NX) + (c + dc) % 2]
-        return copy(slot, slot, g_s.at[dx, dc], g_r.at[dx, dc], sibling)
-
-    for dx, dc in partners:
-        g_copy(dx, dc).start()
-    att[2 * x + c] = own_att[c]
-
-    def w_step(n, _):
+    def arrive_pair(p):
+        arrive(2 * p)
+        arrive(2 * p + 1)
+
+    def hop(p, _):
+        arrive_pair(p)
+        return 0
+
+    def w_step(n):
         d = 1 + n // 2
         s = n % 2
         r = (1 - s) * (NZ - d) + s * d
@@ -303,9 +281,63 @@
             w_copy(r, r - 1 + 2 * s, 1 + 6 * s).start()
 
         w_share(r).start()
-        return 0
-
-    lax.fori_loop(0, 6, w_step, 0)
+
+    lax.fori_loop(0, 4, hop, 0)
+    for dx, dc in partners:
+        q_arrival(dx, dc).wait_recv()
+    def first_unit(step):
+        return step + (jnp.minimum(step, 3) + 1) // 2
+
+    def ring_step(step, _):
+        @pl.when(step < 8)
+        def _():
+            arrive_pair(step + 4)
+
+        @pl.when(step == 8)
+        def _():
+            w_step(0)
+            w_step(1)
+
+        @pl.when((step >= 8) & (step < 12))
+        def _():
+            block = block_of(step - 8, 4)
+            copy(block, block, z_s.at[step - 8, 4], z_r.at[step - 8, 4], sibling).wait_recv()
+            share_copy(step - 8, 4).start()
+
+        @pl.when(step == 12)
+        def _():
+            w_step(2)
+            w_step(3)
+
+        lax.fori_loop(first_unit(step), first_unit(step + 1), attend_unit, 0)
+        return 0
+
+    lax.fori_loop(0, 14, ring_step, 0)
+
+    def finish(row, _):
+        total = jnp.sum(l_ref[row], axis=1, keepdims=True)
+        done = (acc_ref[row] / total).astype(jnp.bfloat16)
+        own_att[0, row] = done[:ROWS]
+        own_att[1, row] = done[ROWS:]
+        return 0
+
+    lax.fori_loop(0, NX, finish, 0)
+
+    def g_copy(dx, dc):
+        return copy(
+            own_att.at[(c + dc) % 2], att.at[2 * x + c], g_s.at[dx, dc], g_r.at[dx, dc], device(dx, 0, dc)
+        )
+
+    def g_arrival(dx, dc):
+        slot = att.at[2 * ((x + NX - dx) % NX) + (c + dc) % 2]
+        return copy(slot, slot, g_s.at[dx, dc], g_r.at[dx, dc], sibling)
+
+    for dx, dc in partners:
+        g_copy(dx, dc).start()
+    att[2 * x + c] = own_att[c]
+
+    w_step(4)
+    w_step(5)
     last_w = wbuf.at[(z + 4) % NZ, c]
     copy(last_w, last_w, w_s.at[4], w_r.at[4], sibling).wait_recv()
     w_share(4).start()
@@ -406,16 +438,20 @@
 
 
 def shards(queries, keys, values, out_weight, doc_lengths):
-    cosine, sine = rotary_tables(doc_lengths)
     vmem = pl.BlockSpec(memory_space=pltpu.VMEM)
+    hbm = pl.BlockSpec(memory_space=pltpu.HBM)
     bf16, f32 = jnp.bfloat16, jnp.float32
     dma = pltpu.SemaphoreType.DMA
     return pl.pallas_call(
         kernel,
         out_shape=jax.ShapeDtypeStruct((ROWS, 1024), bf16),
-        in_specs=[vmem] * 6 + [pl.BlockSpec(memory_space=pltpu.SMEM)],
+        in_specs=[hbm] * 4 + [vmem, pl.BlockSpec(memory_space=pltpu.SMEM)],
         out_specs=vmem,
         scratch_shapes=[
+            pltpu.VMEM((ROWS, 1024), bf16),
+            pltpu.VMEM((ROWS, 256), bf16),
+            pltpu.VMEM((ROWS, 256), bf16),
+            dma((4,)),
             pltpu.VMEM((8, ROWS, HD), bf16),
             pltpu.VMEM((2, 2, ROWS, HD), bf16),
             pltpu.VMEM((NX, 2, ROWS, HD), bf16),
@@ -439,9 +475,9 @@
             dma((4, 4)), dma((4, 4)),
         ],
         compiler_params=pltpu.CompilerParams(
-            collective_id=0, has_side_effects=True, vmem_limit_bytes=48 << 20
+            collective_id=0, has_side_effects=True, vmem_limit_bytes=56 << 20
         ),
-    )(queries, keys, values, out_weight.T, cosine, sine, doc_lengths)
+    )(queries, keys, values, out_weight.T, jnp.asarray(frequencies()), doc_lengths)
 
 
 def solution(mesh):

time: 90.5 us -> 73.8 us (0.82)
  Pallas kernels: 80 us -> 71.6 us
  between operations: 3.81 us -> 0.01 us
  local copies, waits for them, and re-layouts: 4.67 us -> 1.67 us
  other arithmetic: 1.76 us -> 0 us
    pallas_call x1, Pallas kernels: 80 us -> 71.6 us  [shards(): pl.pallas_call(kernel, out_shape=jax.ShapeDtypeStruct((ROWS, 1024), bf16)...]
    select_n x2 -> x0, other arithmetic: 1.74 us -> none  [the longest x1 1.11 us: rotary_tables(): return (jnp.cos(angles), jnp.where(lane < half, -sine, sine))]
    slice x1 -> x0, local copies, waits for them, and re-layouts: 1.53 us -> none  [rotary_tables(): end = end + doc_lengths[number]]
    unnamed x11 -> x1, local copies, waits for them, and re-layouts: 3.13 us -> 1.67 us
where the time goes in v2:
time: 73.8 us; the launch traced here: 73.3 us
  Pallas kernels  71.6 us (97%)
  local copies, waits for them, and re-layouts  1.67 us (2%)
    pallas_call x1, Pallas kernels, shards(): pl.pallas_call(kernel, out_shape=jax.ShapeDtypeStruct((ROWS, 1024), bf16)...  71.6 us
    unnamed x1, local copies, waits for them, and re-layouts  1.67 us

profile of v2, /device:TPU:4, one launch (start us, length us, event | category | flops | bytes accessed | tf_op | source)
XLA Modules:
  0.0 73.3 jit_solution(17196147251774438219)
XLA Ops:
  0.0 71.6 %shard_map.64 = bf16[128,1024]{1,0:T(8,128)(2,1)} custom-call(bf16[128,1024]{1,0:T(8,128)(2,1)} %q_hbm.1, bf16[128,256]{1,0:T(8,128)(2,1)} %k_hbm.1, bf16[128,256]{1,0:T(8,128)(2,1)} %v_hbm.1, bf16[64,1024]{1,0:T(8,128)(2,1)} %bitcast.1, f32[1,128]{1,0:T(1,128)} %constant.2.clone.freq_ref, s32[6]{0:T(128)} %len_ref.1), custom_call_target="tpu_custom_call" | custom-call | tf_op jit(solution)/shard_map/pallas_call | solution.py:445
  71.6 1.7 %copy.8 = bf16[128,1024]{1,0:T(8,128)(2,1)} copy(bf16[128,1024]{1,0:T(8,128)(2,1)} %shard_map.64) | data formatting | bytes 524288

commit v3 on v2

--- a/solution.py
+++ b/solution.py
@@ -25,8 +25,8 @@
 
 
 def kernel(
-    q_hbm, k_hbm, v_hbm, w_hbm, freq_ref, len_ref, out_ref,
-    q_in, k_in, v_in, in_sem, q_stage, kv_stage, qbuf, kv, start_ref, m_ref, l_ref, acc_ref, own_att, att, wbuf, pbuf, part,
+    q_hbm, k_hbm, v_hbm, w_hbm, freq_hbm, len_hbm, out_ref,
+    freq_ref, len_ref, q_in, k_in, v_in, in_sem, q_stage, kv_stage, qbuf, kv, start_ref, m_ref, l_ref, acc_ref, own_att, att, wbuf, pbuf, part,
     a_s, a_r, q_s, q_r, z_s, z_r, sh_s, sh_r, g_s, g_r, w_s, w_r, wsh_s, wsh_r, e_s, e_r,
 ):
     t = lax.axis_index("tok")
@@ -39,15 +39,6 @@
         return (((x + dx) % NX) * 16 + ((z + dz) % NZ) * 2 + (c + dc) % 2, y)
 
     sibling = device(0, 0, 1)
-
-    loads = [
-        pltpu.make_async_copy(k_hbm, k_in, in_sem.at[0]),
-        pltpu.make_async_copy(v_hbm, v_in, in_sem.at[1]),
-        pltpu.make_async_copy(q_hbm, q_in, in_sem.at[2]),
-        pltpu.make_async_copy(w_hbm, wbuf.at[z, c], in_sem.at[3]),
-    ]
-    for load in loads:
-        load.start()
 
     barrier = pltpu.get_barrier_semaphore()
     count = 0
@@ -66,11 +57,24 @@
         greet(device(0, dz, 0))
         count += 1
 
+    loads = [
+        pltpu.make_async_copy(k_hbm, k_in, in_sem.at[0]),
+        pltpu.make_async_copy(v_hbm, v_in, in_sem.at[1]),
+        pltpu.make_async_copy(q_hbm, q_in, in_sem.at[2]),
+        pltpu.make_async_copy(w_hbm, wbuf.at[z, c], in_sem.at[3]),
+        pltpu.make_async_copy(freq_hbm, freq_ref, in_sem.at[4]),
+        pltpu.make_async_copy(len_hbm, len_ref, in_sem.at[5]),
+    ]
+    for load in loads:
+        load.start()
+
     def copy(src, dst, send, recv, who):
         return pltpu.make_async_remote_copy(
             src_ref=src, dst_ref=dst, send_sem=send, recv_sem=recv, device_id=who, device_id_type=MESH
         )
 
+    loads[4].wait()
+    loads[5].wait()
     ends = []
     end = len_ref[0]
     for number in range(5):
@@ -442,16 +446,19 @@
     hbm = pl.BlockSpec(memory_space=pltpu.HBM)
     bf16, f32 = jnp.bfloat16, jnp.float32
     dma = pltpu.SemaphoreType.DMA
+    operands = (queries, keys, values, out_weight.T, jnp.asarray(frequencies()), doc_lengths)
     return pl.pallas_call(
         kernel,
         out_shape=jax.ShapeDtypeStruct((ROWS, 1024), bf16),
-        in_specs=[hbm] * 4 + [vmem, pl.BlockSpec(memory_space=pltpu.SMEM)],
+        in_specs=[hbm] * 6,
         out_specs=vmem,
         scratch_shapes=[
+            pltpu.VMEM((1, HD), f32),
+            pltpu.SMEM((6,), jnp.int32),
             pltpu.VMEM((ROWS, 1024), bf16),
             pltpu.VMEM((ROWS, 256), bf16),
             pltpu.VMEM((ROWS, 256), bf16),
-            dma((4,)),
+            dma((6,)),
             pltpu.VMEM((8, ROWS, HD), bf16),
             pltpu.VMEM((2, 2, ROWS, HD), bf16),
             pltpu.VMEM((NX, 2, ROWS, HD), bf16),
@@ -475,9 +482,9 @@
             dma((4, 4)), dma((4, 4)),
         ],
         compiler_params=pltpu.CompilerParams(
-            collective_id=0, has_side_effects=True, vmem_limit_bytes=56 << 20
+            collective_id=0, has_side_effects=True, vmem_limit_bytes=48 << 20
         ),
-    )(queries, keys, values, out_weight.T, jnp.asarray(frequencies()), doc_lengths)
+    )(*(pltpu.with_memory_space_constraint(array, pltpu.HBM) for array in operands))
 
 
 def solution(mesh):

time: 73.8 us -> 71.2 us (0.965)
  Pallas kernels: 71.6 us -> 70.1 us
  local copies, waits for them, and re-layouts: 1.67 us -> 0.71 us
    pallas_call x1, Pallas kernels: 71.6 us -> 70.1 us  [shards(): pl.pallas_call(kernel, out_shape=jax.ShapeDtypeStruct((ROWS, 1024), bf16)...]
    unnamed x1, local copies, waits for them, and re-layouts: 1.67 us -> 0.71 us
where the time goes in v3:
time: 71.2 us; the launch traced here: 70.8 us
  Pallas kernels  70.1 us (98%)
    pallas_call x1, Pallas kernels, shards(): pl.pallas_call(kernel, out_shape=jax.ShapeDtypeStruct((ROWS, 1024), bf16)...  70.1 us

profile of v3, /device:TPU:4, one launch (start us, length us, event | category | flops | bytes accessed | tf_op | source)
XLA Modules:
  0.0 70.8 jit_solution(13219285524574313229)
XLA Ops:
  0.0 70.1 %shard_map.64 = bf16[128,1024]{1,0:T(8,128)(2,1)S(1)} custom-call(bf16[128,1024]{1,0:T(8,128)(2,1)} %q_hbm.1, bf16[128,256]{1,0:T(8,128)(2,1)} %k_hbm.1, bf16[128,256]{1,0:T(8,128)(2,1)} %v_hbm.1, bf16[64,1024]{1,0:T(8,128)(2,1)} %bitcast.1, f32[1,128]{1,0:T(1,128)} %constant.2.clone.freq_hbm, s32[6]{0:T(128)} %len_hbm.1), custom_call_target="tpu_custom_call" | custom-call | tf_op jit(solution)/shard_map/pallas_call | solution.py:450
  70.1 0.7 copy.8

commit v4 on v3

--- a/solution.py
+++ b/solution.py
@@ -327,27 +327,43 @@
 
     lax.fori_loop(0, NX, finish, 0)
 
-    def g_copy(dx, dc):
+    def g_slot(dx, dc, half):
+        return att.at[2 * ((x + NX - dx) % NX) + (c + dc) % 2, 2 * half : 2 * half + 2]
+
+    def g_copy(dx, dc, half):
+        block = own_att.at[(c + dc) % 2, 2 * half : 2 * half + 2]
         return copy(
-            own_att.at[(c + dc) % 2], att.at[2 * x + c], g_s.at[dx, dc], g_r.at[dx, dc], device(dx, 0, dc)
+            block, g_slot(0, 0, half), g_s.at[dx, dc, half], g_r.at[dx, dc, half], device(dx, 0, dc)
         )
 
-    def g_arrival(dx, dc):
-        slot = att.at[2 * ((x + NX - dx) % NX) + (c + dc) % 2]
-        return copy(slot, slot, g_s.at[dx, dc], g_r.at[dx, dc], sibling)
-
-    for dx, dc in partners:
-        g_copy(dx, dc).start()
+    def g_forward(dc, half):
+        slot = g_slot(1 + 2 * half, dc, half)
+        return copy(
+            slot, slot, g_s.at[2, dc, half], g_r.at[2, dc, half], device(1 + 2 * half, 0, 0)
+        )
+
+    def g_arrival(dx, dc, half):
+        slot = g_slot(dx, dc, half)
+        return copy(slot, slot, g_s.at[dx, dc, half], g_r.at[dx, dc, half], sibling)
+
+    onward = [(1, 0, 0), (3, 0, 1), (1, 1, 0), (3, 1, 1)]
+    near = [(1, 0, 1), (3, 0, 0), (1, 1, 1), (3, 1, 0), (0, 1, 0), (0, 1, 1)]
+    far = [(2, 0, 0), (2, 0, 1), (2, 1, 0), (2, 1, 1)]
+    for place in onward + near:
+        g_copy(*place).start()
     att[2 * x + c] = own_att[c]
-
     w_step(4)
     w_step(5)
+    for dx, dc, half in onward:
+        g_arrival(dx, dc, half).wait_recv()
+        g_forward(dc, half).start()
+
     last_w = wbuf.at[(z + 4) % NZ, c]
     copy(last_w, last_w, w_s.at[4], w_r.at[4], sibling).wait_recv()
     w_share(4).start()
 
-    for dx, dc in partners:
-        g_arrival(dx, dc).wait_recv()
+    for place in near + far:
+        g_arrival(*place).wait_recv()
 
     def w_wait(r, _):
         w_share_arrival(r).wait_recv()
@@ -401,7 +417,10 @@
         x_copy(dx).wait_send()
     for dx, dc in partners:
         q_copy(dx, dc).wait_send()
-        g_copy(dx, dc).wait_send()
+    for place in onward + near:
+        g_copy(*place).wait_send()
+    for _, dc, half in far:
+        g_forward(dc, half).wait_send()
 
     def sent(n, _):
         j = n % 4
@@ -476,7 +495,7 @@
             dma((4, 2)), dma((4, 2)),
             dma((4, 8)), dma((4, 8)),
             dma((4, 8)), dma((4, 8)),
-            dma((4, 2)), dma((4, 2)),
+            dma((4, 2, 2)), dma((4, 2, 2)),
             dma((8,)), dma((8,)),
             dma((8,)), dma((8,)),
             dma((4, 4)), dma((4, 4)),

time: 71.2 us -> 68.4 us (0.961)
  Pallas kernels: 70.1 us -> 67.6 us
    pallas_call x1, Pallas kernels: 70.1 us -> 67.6 us  [shards(): pl.pallas_call(kernel, out_shape=jax.ShapeDtypeStruct((ROWS, 1024), bf16)...]
where the time goes in v4:
time: 68.4 us; the launch traced here: 68.3 us
  Pallas kernels  67.6 us (99%)
  local copies, waits for them, and re-layouts  0.71 us (1%)
    pallas_call x1, Pallas kernels, shards(): pl.pallas_call(kernel, out_shape=jax.ShapeDtypeStruct((ROWS, 1024), bf16)...  67.6 us

profile of v4, /device:TPU:4, one launch (start us, length us, event | category | flops | bytes accessed | tf_op | source)
XLA Modules:
  0.0 68.3 jit_solution(8924855387270808357)
XLA Ops:
  0.0 67.6 %shard_map.64 = bf16[128,1024]{1,0:T(8,128)(2,1)S(1)} custom-call(bf16[128,1024]{1,0:T(8,128)(2,1)} %q_hbm.1, bf16[128,256]{1,0:T(8,128)(2,1)} %k_hbm.1, bf16[128,256]{1,0:T(8,128)(2,1)} %v_hbm.1, bf16[64,1024]{1,0:T(8,128)(2,1)} %bitcast.1, f32[1,128]{1,0:T(1,128)} %constant.2.clone.freq_hbm, s32[6]{0:T(128)} %len_hbm.1), custom_call_target="tpu_custom_call" | custom-call | tf_op jit(solution)/shard_map/pallas_call | solution.py:469
  67.6 0.7 %copy.8 = bf16[128,1024]{1,0:T(8,128)(2,1)} copy(bf16[128,1024]{1,0:T(8,128)(2,1)S(1)} %shard_map.64) | data formatting | bytes 524288

commit v5 on v4

--- a/solution.py
+++ b/solution.py
@@ -399,20 +399,6 @@
 
     lax.fori_loop(0, 4, project, 0)
 
-    for nb in range(4):
-        for source in range(NY):
-            slot = part.at[source, nb]
-            arrival = copy(slot, slot, e_s.at[source, nb], e_r.at[source, nb], sibling)
-
-            @pl.when(jnp.logical_not((x == y) & (source == y)))
-            def _():
-                arrival.wait_recv()
-
-        total = part[0, nb].astype(jnp.float32)
-        for source in range(1, NY):
-            total = total + part[source, nb].astype(jnp.float32)
-        out_ref[:, nb * 256 : (nb + 1) * 256] = total.astype(jnp.bfloat16)
-
     for dx in (1, 3, 2):
         x_copy(dx).wait_send()
     for dx, dc in partners:
@@ -451,6 +437,20 @@
         return 0
 
     lax.fori_loop(1, NZ, w_ring_sent, 0)
+    for nb in range(4):
+        for source in range(NY):
+            slot = part.at[source, nb]
+            arrival = copy(slot, slot, e_s.at[source, nb], e_r.at[source, nb], sibling)
+
+            @pl.when(jnp.logical_not((x == y) & (source == y)))
+            def _():
+                arrival.wait_recv()
+
+        total = part[0, nb].astype(jnp.float32)
+        for source in range(1, NY):
+            total = total + part[source, nb].astype(jnp.float32)
+        out_ref[:, nb * 256 : (nb + 1) * 256] = total.astype(jnp.bfloat16)
+
     for row in range(NX):
         mine = (x == row) & (y == x)
 

time: 68.4 us -> 67.5 us (0.987)
  Pallas kernels: 67.6 us -> 66.7 us
    pallas_call x1, Pallas kernels: 67.6 us -> 66.7 us  [shards(): pl.pallas_call(kernel, out_shape=jax.ShapeDtypeStruct((ROWS, 1024), bf16)...]
where the time goes in v5:
time: 67.5 us; the launch traced here: 67.4 us
  Pallas kernels  66.7 us (99%)
  local copies, waits for them, and re-layouts  0.71 us (1%)
    pallas_call x1, Pallas kernels, shards(): pl.pallas_call(kernel, out_shape=jax.ShapeDtypeStruct((ROWS, 1024), bf16)...  66.7 us

profile of v5, /device:TPU:4, one launch (start us, length us, event | category | flops | bytes accessed | tf_op | source)
XLA Modules:
  0.0 67.4 jit_solution(17980939330784670016)
XLA Ops:
  0.0 66.7 %shard_map.64 = bf16[128,1024]{1,0:T(8,128)(2,1)S(1)} custom-call(bf16[128,1024]{1,0:T(8,128)(2,1)} %q_hbm.1, bf16[128,256]{1,0:T(8,128)(2,1)} %k_hbm.1, bf16[128,256]{1,0:T(8,128)(2,1)} %v_hbm.1, bf16[64,1024]{1,0:T(8,128)(2,1)} %bitcast.1, f32[1,128]{1,0:T(1,128)} %constant.2.clone.freq_hbm, s32[6]{0:T(128)} %len_hbm.1), custom_call_target="tpu_custom_call" | custom-call | tf_op jit(solution)/shard_map/pallas_call | solution.py:469
  66.7 0.7 %copy.8 = bf16[128,1024]{1,0:T(8,128)(2,1)} copy(bf16[128,1024]{1,0:T(8,128)(2,1)S(1)} %shard_map.64) | data formatting | bytes 524288

commit v6 on v5

--- a/solution.py
+++ b/solution.py
@@ -308,7 +308,7 @@
             copy(block, block, z_s.at[step - 8, 4], z_r.at[step - 8, 4], sibling).wait_recv()
             share_copy(step - 8, 4).start()
 
-        @pl.when(step == 12)
+        @pl.when(step == 13)
         def _():
             w_step(2)
             w_step(3)

time: 67.5 us -> 67.6 us (level)
  no operation moved by 1% of the time
where the time goes in v6:
time: 67.6 us; the launch traced here: 67.5 us
  Pallas kernels  66.8 us (99%)
  local copies, waits for them, and re-layouts  0.71 us (1%)
    pallas_call x1, Pallas kernels, shards(): pl.pallas_call(kernel, out_shape=jax.ShapeDtypeStruct((ROWS, 1024), bf16)...  66.8 us

profile of v6, /device:TPU:4, one launch (start us, length us, event | category | flops | bytes accessed | tf_op | source)
XLA Modules:
  0.0 67.5 jit_solution(4475231806527044103)
XLA Ops:
  0.0 66.8 %shard_map.64 = bf16[128,1024]{1,0:T(8,128)(2,1)S(1)} custom-call(bf16[128,1024]{1,0:T(8,128)(2,1)} %q_hbm.1, bf16[128,256]{1,0:T(8,128)(2,1)} %k_hbm.1, bf16[128,256]{1,0:T(8,128)(2,1)} %v_hbm.1, bf16[64,1024]{1,0:T(8,128)(2,1)} %bitcast.1, f32[1,128]{1,0:T(1,128)} %constant.2.clone.freq_hbm, s32[6]{0:T(128)} %len_hbm.1), custom_call_target="tpu_custom_call" | custom-call | tf_op jit(solution)/shard_map/pallas_call | solution.py:469
  66.8 0.7 %copy.8 = bf16[128,1024]{1,0:T(8,128)(2,1)} copy(bf16[128,1024]{1,0:T(8,128)(2,1)S(1)} %shard_map.64) | data formatting | bytes 524288
